TPU v7x, 256 devices: a whole 4x4x8 slice. The times are simulated.
256 devices in a mesh: chan: 32 (over z_lo, x, core), inp: 8 (over z_hi, y).
Axes of the slice: x: 4, y: 4, z: 8 (z_hi: 2, z_lo: 4; z = z_hi * 4 + z_lo), core: 2. Of those that a mesh axis runs over, the one named last changes fastest.
Arguments:
- voltages: bfloat16 [512, 2, 131072], P('inp', None, 'chan'), may hold values from -64 to 64
Outputs:
- delays: float32 [512, 512, 2, 512], P('inp', 'chan')
All inputs are finite; a program needn't handle non-finite values.
Results may differ from a plain program's by a relative error of at most 0.0053.
Values may be sent and summed in bfloat16 or wider, within the bound.
No kernel may reach another device: no remote copies, remote signals or barrier semaphores. Data moves between devices by JAX's collectives and lax.ppermute only.
A program may use at most 128 MiB of HBM per device.

v0:
```python
import math
import jax
import jax.numpy as jnp
from jax import lax
from jax.sharding import PartitionSpec as P

NCH = 512


def taper_weights(count):
    position = jnp.arange(count, dtype=jnp.float32)
    return 0.5 - 0.5 * jnp.cos(2.0 * math.pi * (position + 0.5) / count)


def channel_table(count):
    indices = jnp.arange(count, dtype=jnp.int32)
    product = indices[:, None] * indices[None, :] % count
    angle = 2.0 * math.pi / count * product.astype(jnp.float32)
    window = taper_weights(count)[:, None] / math.sqrt(count)
    cosine = window * jnp.cos(angle)
    sine = window * jnp.sin(angle)
    upper = jnp.concatenate([cosine, -sine], axis=1)
    lower = jnp.concatenate([sine, cosine], axis=1)
    return jnp.concatenate([upper, lower], axis=0).astype(jnp.bfloat16)


def dft_tables(row_count, col_count, modulus):
    row_idx = jnp.arange(row_count, dtype=jnp.int32)
    col_idx = jnp.arange(col_count, dtype=jnp.int32)
    angle = (
        2.0
        * math.pi
        / modulus
        * (row_idx[:, None] * col_idx[None, :] % modulus).astype(jnp.float32)
    )
    return (jnp.cos(angle), jnp.sin(angle))


def complex_section(real_in, imag_in, cosine, sine, form):
    highest = lax.Precision.HIGHEST
    real_out = jnp.einsum(form, cosine, real_in, precision=highest) + jnp.einsum(
        form, sine, imag_in, precision=highest
    )
    imag_out = jnp.einsum(form, cosine, imag_in, precision=highest) - jnp.einsum(
        form, sine, real_in, precision=highest
    )
    return (real_out, imag_out)


def rotate(real_in, imag_in, cosine, sine):
    return (real_in * cosine + imag_in * sine, imag_in * cosine - real_in * sine)


def shards(voltages):
    input_rows = voltages.shape[0]
    local_time = voltages.shape[2]
    chan_count = lax.axis_size("chan")
    spec_local = local_time // NCH
    chan_local = NCH // chan_count
    table = channel_table(NCH)
    table = (
        table.reshape(2 * NCH, 2, chan_local, chan_count)
        .transpose(0, 1, 3, 2)
        .reshape(2 * NCH, 2 * NCH)
    )
    samples = (
        voltages.reshape(input_rows, 2, spec_local, NCH)
        .transpose(0, 2, 1, 3)
        .reshape(input_rows * spec_local, 2 * NCH)
    )
    spectra = jnp.dot(samples, table, preferred_element_type=jnp.float32).astype(jnp.bfloat16)
    spectra = spectra.reshape(input_rows, spec_local, 2, NCH)
    turned = lax.all_to_all(spectra, "chan", split_axis=3, concat_axis=1, tiled=True)
    spec_total = turned.shape[1]
    mine = turned.transpose(3, 0, 2, 1).reshape(chan_local, input_rows, 2 * spec_total)
    own_power = jnp.sum(jnp.square(mine.astype(jnp.float32)), axis=2) / spec_total + 1e-06
    own_scale = lax.rsqrt(own_power)
    piece = lax.all_gather(mine, "inp", axis=1, tiled=True)
    half = piece.shape[2] // 2
    rotated = jnp.concatenate([-piece[:, :, half:], piece[:, :, :half]], axis=2)
    numbers = (((2,), (2,)), ((0,), (0,)))
    real_part = lax.dot_general(mine, piece, numbers, preferred_element_type=jnp.float32)
    imag_part = lax.dot_general(mine, rotated, numbers, preferred_element_type=jnp.float32)
    power = jnp.sum(jnp.square(piece.astype(jnp.float32)), axis=2) / spec_total + 1e-06
    scaling = own_scale[:, :, None] * lax.rsqrt(power)[:, None, :] / spec_total
    rho = jnp.stack([real_part * scaling, imag_part * scaling], axis=1).astype(jnp.bfloat16)
    col_local = rho.shape[3] // chan_count
    baseline_count = input_rows * col_local
    chan_index = lax.axis_index("chan")
    position = (chan_count * jnp.arange(chan_local, dtype=jnp.int32) + chan_index).astype(
        jnp.float32
    )
    taper_local = 0.5 - 0.5 * jnp.cos(2.0 * math.pi * (position + 0.5) / NCH)
    weighted = rho.astype(jnp.float32) * taper_local[:, None, None, None]
    cos_first, sin_first = dft_tables(chan_local, chan_local, chan_local)
    section_real, section_imag = complex_section(
        weighted[:, 0], weighted[:, 1], cos_first, sin_first, "ka,aij->kij"
    )
    twist = (
        2.0
        * math.pi
        / NCH
        * (chan_index * jnp.arange(chan_local, dtype=jnp.int32) % NCH).astype(jnp.float32)
    )
    section_real, section_imag = rotate(
        section_real, section_imag, jnp.cos(twist)[:, None, None], jnp.sin(twist)[:, None, None]
    )
    paired = jnp.stack([section_real, section_imag], axis=1)
    arranged = paired.reshape(chan_local, 2, input_rows, chan_count, col_local).transpose(
        3, 0, 1, 2, 4
    )
    arranged = arranged.reshape(chan_count, chan_local, 2, baseline_count)
    regrouped = lax.all_to_all(arranged, "chan", split_axis=0, concat_axis=0, tiled=True)
    cos_second, sin_second = dft_tables(chan_count, chan_count, chan_count)
    out_real, out_imag = complex_section(
        regrouped[:, :, 0], regrouped[:, :, 1], cos_second, sin_second, "mb,bkn->mkn"
    )
    factor = math.sqrt(spec_total / NCH)
    combined = (
        jnp.stack(
            [out_real.reshape(NCH, baseline_count), out_imag.reshape(NCH, baseline_count)], axis=0
        )
        * factor
    )
    result = combined.transpose(2, 0, 1).reshape(input_rows, col_local, 2, NCH)
    rows_global = lax.axis_index("inp") * input_rows + jnp.arange(input_rows, dtype=jnp.int32)
    cols_global = lax.axis_index("chan") * col_local + jnp.arange(col_local, dtype=jnp.int32)
    same = rows_global[:, None] == cols_global[None, :]
    return jnp.where(same[:, :, None, None], jnp.zeros_like(result), result)


def solution(mesh):
    in_specs = (P("inp", None, "chan"),)
    out_specs = P("inp", "chan", None, None)
    return jax.shard_map(shards, mesh=mesh, in_specs=in_specs, out_specs=out_specs, check_vma=False)
```

profile of v0, /device:TPU:1, one launch (start us, length us, event | category | flops | bytes accessed | tf_op | source)
XLA Modules:
  0.0 456.4 jit_solution(16119081496924792960)
XLA Ops:
  8.4 4.7 %negate_convert_fusion = (bf16[512,1,16,32]{0,2,3,1:T(8,128)(2,1)S(1)}, bf16[512,1,16,32]{0,2,3,1:T(8,128)(2,1)S(1)}, bf16[512,1,16,32]{0,2,3,1:T(8,128)(2,1)S(1)}) fusion(s32[16,32]{0,1:T(8,128)S(1)} %multiply_add_fusion.1, f32[512]{0:T(512)S(1)} %subtract_multiply_fusion), kind=kLoop, calls=%fused_computation.48 | loop fusion | flops 5242880 | bytes 1576960 | tf_op jit(solution)/shard_map/convert.9
  16.0 2.9 copy.58
  20.4 36.5 %all_to_all.23 = bf16[32,2,8192]{2,1,0:T(2,128)(2,1)S(1)} all-to-all(bf16[32,2,8192]{2,1,0:T(2,128)(2,1)S(1)} %reshape.207), channel_id=1, replica_groups=mesh['chan'=32,'inp'=8] {'chan'}, dimensions={0} | all-to-all | bytes 2097152 | tf_op jit(solution)/shard_map/all_to_all | solution.py:73
  61.3 2.7 copy.61
  66.4 170.8 %all-gather.2.cloned.1.call-done = bf16[16,512,512]{2,1,0:T(8,128)(2,1)} async-done(((bf16[16,64,512]{2,1,0:T(8,128)(2,1)}), bf16[16,512,512]{2,1,0:T(8,128)(2,1)}) %all-gather.2.cloned.1.call-update) | async-done | bytes 8388624 | tf_op jit(solution)/shard_map/all_gather | solution.py:78
  237.1 5.3 %multiply_reduce_fusion = f32[16,512]{1,0:T(8,128)S(1)} fusion(bf16[16,512,512]{2,1,0:T(8,128)(2,1)} %all-gather.2.cloned.1.call-done), kind=kLoop, calls=%fused_computation | loop fusion | flops 12574720 | bytes 8421376 | tf_op jit(solution)/shard_map/reduce_sum | solution.py:84
  244.1 3.0 fusion.29
  251.2 2.9 fusion.11
  254.1 2.9 fusion.9
  257.0 2.9 fusion.17
  259.9 17.3 %multiply_add_fusion = (f32[16,64,512]{2,0,1:T(8,128)}, f32[16,64,512]{2,0,1:T(8,128)S(1)}) fusion(f32[16,64,512]{2,0,1:T(8,128)S(1)} %fusion.17, f32[16]{0:T(128)S(1)} %get-tuple-element.16, f32[16]{0:T(128)S(1)} %get-tuple-element.17, f32[16,64,512]{2,0,1:T(8,128)S(1)} %fusion.9, f32[16,64,512]{2,1,0:T(8,128)S(1)} %get-tuple-element.11), kind=kOutput, calls=%fused_computation.17 | convolution fusion | flops 104336896 | bytes 10485888 | tf_op jit(solution)/shard_map/ka,aij->kij/dot_general | solution.py:44
  277.3 3.8 copy.66
  281.1 2.8 copy.67
  283.8 7.6 %maximum_bitcast_fusion = f32[32,16,2,64,16]{3,4,0,1,2:T(8,128)} fusion(f32[16,1,64,32,16]{2,4,3,0,1:T(8,128)} %bitcast.78, f32[16,1,64,32,16]{2,4,3,0,1:T(8,128)} %bitcast.77), kind=kLoop, calls=%fused_computation.5 | loop fusion | flops 1048576 | bytes 8388608 | tf_op jit(solution)/shard_map/transpose | solution.py:109
  291.5 13.4 %copy.68 = f32[32,16,2,64,16]{0,4,3,2,1:T(8,128)} copy(f32[32,16,2,64,16]{3,4,0,1,2:T(8,128)} %maximum_bitcast_fusion) | data formatting | bytes 8388608 | tf_op jit(solution)/shard_map/transpose | solution.py:109
  304.8 11.7 %copy.69 = f32[32,16,2,1024]{3,1,2,0:T(8,128)} copy(f32[32,16,2,1024]{0,3,2,1:T(8,128)} %bitcast.74) | data formatting | bytes 8388608 | tf_op jit(solution)/shard_map/reshape | solution.py:112
  316.6 5.9 %all-to-all-start.1 = ((f32[32,16,2,1024]{3,1,2,0:T(8,128)}), f32[32,16,2,1024]{3,1,2,0:T(8,128)}, u32[]{:S(2)}, u32[]{:S(2)}) async-start(f32[32,16,2,1024]{3,1,2,0:T(8,128)} %copy.69), calls=%async_computation.1 | async-start | bytes 8388608 | tf_op jit(solution)/shard_map/all_to_all | solution.py:113
  322.5 93.0 %all-to-all-done.1 = f32[32,16,2,1024]{3,1,2,0:T(8,128)} async-done(((f32[32,16,2,1024]{3,1,2,0:T(8,128)}), f32[32,16,2,1024]{3,1,2,0:T(8,128)}, u32[]{:S(2)}, u32[]{:S(2)}) %all-to-all-start.1) | async-done | bytes 4194336 | tf_op jit(solution)/shard_map/all_to_all | solution.py:113
  418.1 3.0 fusion.6
  421.2 3.0 fusion.5
  424.2 3.0 fusion.23
  428.4 3.2 fusion.24
  435.4 5.4 %copy.74 = f32[1024,2,512]{2,0,1:T(8,128)} copy(f32[1024,2,512]{0,2,1:T(8,128)} %fusion.4) | data formatting | bytes 8388608 | tf_op jit(solution)/shard_map/transpose | solution.py:125
  443.3 5.8 %copy.75 = f32[64,16,2,512]{3,2,1,0:T(2,128)} copy(f32[64,16,2,512]{3,1,0,2:T(8,128)S(1)} %broadcast_select_fusion) | data formatting | bytes 8388608 | tf_op jit(solution)/shard_map/jit(_where)/select_n | solution.py:129
  (34 shorter events, 28.9 us)
Async XLA Ops:
  6.5 230.6 %all-gather.2.cloned.1.call-start = ((), (), s32[]{:S(2)}) async-start(), calls=%async_computation.2 | async-start | bytes 9437184 | tf_op jit(solution)/shard_map/all_gather | solution.py:78
  237.1 5.8 %copy-start = (bf16[16,512,512]{2,1,0:T(8,128)(2,1)S(1)}, bf16[16,512,512]{2,1,0:T(8,128)(2,1)}, u32[]{:S(2)}) copy-start(bf16[16,512,512]{2,1,0:T(8,128)(2,1)} %all-gather.2.cloned.1.call-done) | copy-start | bytes 25165828
  242.9 1.2 copy-start.1
  316.6 99.0 %all-to-all-start.1 = ((f32[32,16,2,1024]{3,1,2,0:T(8,128)}), f32[32,16,2,1024]{3,1,2,0:T(8,128)}, u32[]{:S(2)}, u32[]{:S(2)}) async-start(f32[32,16,2,1024]{3,1,2,0:T(8,128)} %copy.69), calls=%async_computation.1 | async-start | bytes 8388608 | tf_op jit(solution)/shard_map/all_to_all | solution.py:113
Sparse Core Ops, SparseCore 0:
  65.6 171.4 all-gather.1
where the time goes:
time: 465 us; the launch traced here: 456 us
  waiting for transfers between devices  264 us (57%)
  local copies, waits for them, and re-layouts  65.8 us (14%)
  matrix products  45.3 us (10%)
  blocking collectives  36.5 us (8%)
  other arithmetic  25.2 us (5%)
  between operations  14 us (3%)
  starting transfers between devices  5.88 us (1%)
    all_gather x1, waiting for transfers between devices, shards(): piece = lax.all_gather(mine, 'inp', axis=1, tiled=True)  171 us
    all_to_all x1, waiting for transfers between devices, shards(): lax.all_to_all(arranged, 'chan', split_axis=0, concat_axis=0, tiled=True)  93 us
    all_to_all x1, blocking collectives, shards(): lax.all_to_all(spectra, 'chan', split_axis=3, concat_axis=1, tiled=True)  36.5 us
    dot_general x2, matrix products, complex_section(): jnp.einsum(form, sine, real_in, precision=highest)  20.4 us
    transpose x1, local copies, waits for them, and re-layouts, shards(): paired.reshape(chan_local, 2, input_rows, chan_count, col_local)  13.4 us
    reshape x1, local copies, waits for them, and re-layouts, shards(): arranged = arranged.reshape(chan_count, chan_local, 2, baseline_count)  11.7 us
  transfers between devices with their start and end apart: 2, of which 2 were waited for; matrix products, arithmetic and copies ran while one was open for 0% of the time, Pallas kernels for 0%

commit v1 on v0

--- a/solution.py
+++ b/solution.py
@@ -75,7 +75,9 @@
     mine = turned.transpose(3, 0, 2, 1).reshape(chan_local, input_rows, 2 * spec_total)
     own_power = jnp.sum(jnp.square(mine.astype(jnp.float32)), axis=2) / spec_total + 1e-06
     own_scale = lax.rsqrt(own_power)
-    piece = lax.all_gather(mine, "inp", axis=1, tiled=True)
+    piece = jnp.concatenate(
+        lax.all_to_all(jnp.stack([mine] * lax.axis_size("inp")), "inp", 0, 0), axis=1
+    )
     half = piece.shape[2] // 2
     rotated = jnp.concatenate([-piece[:, :, half:], piece[:, :, :half]], axis=2)
     numbers = (((2,), (2,)), ((0,), (0,)))

time: 465 us -> 480 us (1.032)
  waiting for transfers between devices: 264 us -> 279 us
  between operations: 14 us -> 0.45 us
  local copies, waits for them, and re-layouts: 65.8 us -> 79.2 us
  matrix products: 45.3 us -> 33.1 us
  starting transfers between devices: 5.88 us -> 13.8 us
    all_to_all x0 -> x1, waiting for transfers between devices: none -> 186 us  [shards(): lax.all_to_all(jnp.stack([mine] * lax.axis_size('inp')), 'inp', 0, 0)]
    all_gather x1 -> x0, waiting for transfers between devices: 171 us -> none  [shards(): piece = lax.all_gather(mine, 'inp', axis=1, tiled=True)]
    dot_general x2, matrix products: 20.4 us -> 8.17 us  [complex_section(): jnp.einsum(form, sine, real_in, precision=highest)]
    all_to_all x0 -> x1, starting transfers between devices: none -> 8.35 us  [shards(): lax.all_to_all(jnp.stack([mine] * lax.axis_size('inp')), 'inp', 0, 0)]
    reshape x0 -> x1, local copies, waits for them, and re-layouts: none -> 7.71 us  [shards(): jnp.concatenate(lax.all_to_all(jnp.stack([mine] * lax.axis_size('inp')),...]
where the time goes in v1:
time: 480 us; the launch traced here: 470 us
  waiting for transfers between devices  279 us (58%)
  local copies, waits for them, and re-layouts  79.2 us (16%)
  blocking collectives  36.5 us (8%)
  matrix products  33.1 us (7%)
  other arithmetic  28.3 us (6%)
  starting transfers between devices  13.8 us (3%)
    all_to_all x1, waiting for transfers between devices, shards(): lax.all_to_all(jnp.stack([mine] * lax.axis_size('inp')), 'inp', 0, 0)  186 us
    all_to_all x1, waiting for transfers between devices, shards(): lax.all_to_all(arranged, 'chan', split_axis=0, concat_axis=0, tiled=True)  93.1 us
    all_to_all x1, blocking collectives, shards(): lax.all_to_all(spectra, 'chan', split_axis=3, concat_axis=1, tiled=True)  36.5 us
    transpose x1, local copies, waits for them, and re-layouts, shards(): paired.reshape(chan_local, 2, input_rows, chan_count, col_local)  13.4 us
    reshape x1, local copies, waits for them, and re-layouts, shards(): arranged = arranged.reshape(chan_count, chan_local, 2, baseline_count)  11.7 us
  transfers between devices with their start and end apart: 2, of which 2 were waited for; matrix products, arithmetic and copies ran while one was open for 0% of the time, Pallas kernels for 0%

profile of v1, /device:TPU:1, one launch (start us, length us, event | category | flops | bytes accessed | tf_op | source)
XLA Modules:
  0.0 470.3 jit_solution(12760320987310178632)
XLA Ops:
  1.9 4.7 negate_convert_fusion
  13.9 36.5 %all_to_all.28 = bf16[32,2,8192]{2,1,0:T(2,128)(2,1)S(1)} all-to-all(bf16[32,2,8192]{2,1,0:T(2,128)(2,1)S(1)} %reshape.226), channel_id=1, replica_groups=mesh['chan'=32,'inp'=8] {'chan'}, dimensions={0} | all-to-all | bytes 2097152 | tf_op jit(solution)/shard_map/all_to_all | solution.py:73
  54.7 3.0 copy.82
  59.5 4.3 stack.27
  63.8 8.3 %all-to-all-start.1 = ((bf16[8,16,64,512]{3,2,1,0:T(8,128)(2,1)}), bf16[8,16,64,512]{3,2,1,0:T(8,128)(2,1)}, u32[]{:S(2)}, u32[]{:S(2)}) async-start(bf16[8,16,64,512]{3,2,1,0:T(8,128)(2,1)} %stack.27), calls=%async_computation.1 | async-start | bytes 16777216 | tf_op jit(solution)/shard_map/all_to_all | solution.py:79
  73.0 185.8 %all-to-all-done.1 = bf16[8,16,64,512]{3,2,1,0:T(8,128)(2,1)} async-done(((bf16[8,16,64,512]{3,2,1,0:T(8,128)(2,1)}), bf16[8,16,64,512]{3,2,1,0:T(8,128)(2,1)}, u32[]{:S(2)}, u32[]{:S(2)}) %all-to-all-start.1) | async-done | bytes 8388640 | tf_op jit(solution)/shard_map/all_to_all | solution.py:79
  258.9 5.1 %multiply_reduce_fusion = f32[16,8,64]{2,0,1:T(8,128)S(1)} fusion(bf16[8,16,64,512]{3,2,1,0:T(8,128)(2,1)} %all-to-all-done.1), kind=kLoop, calls=%fused_computation | loop fusion | flops 12574720 | bytes 8421376 | tf_op jit(solution)/shard_map/reduce_sum | solution.py:86
  264.1 7.7 %copy.83 = bf16[16,8,64,512]{3,2,1,0:T(8,128)(2,1)} copy(bf16[16,8,64,512]{3,2,0,1:T(8,128)(2,1)} %bitcast.12) | data formatting | bytes 16777216 | tf_op jit(solution)/shard_map/reshape | solution.py:78
  271.8 3.9 slice_negate_fusion
  280.3 3.0 fusion.29
  290.5 2.9 fusion.17
  293.4 5.2 %multiply_add_fusion = (f32[16,64,512]{2,0,1:T(8,128)}, f32[16,64,512]{2,0,1:T(8,128)S(1)}) fusion(f32[16,64,512]{2,0,1:T(8,128)S(1)} %fusion.17, f32[16]{0:T(128)S(1)} %get-tuple-element.17, f32[16]{0:T(128)S(1)} %fusion.75, f32[16,64,512]{2,0,1:T(8,128)S(1)} %fusion.9, f32[16,64,512]{2,1,0:T(8,128)S(1)} %get-tuple-element.11), kind=kOutput, calls=%fused_computation.17 | convolution fusion | flops 104336896 | bytes 10485888 | tf_op jit(solution)/shard_map/ka,aij->kij/dot_general | solution.py:44
  298.6 3.8 copy.89
  305.2 7.6 %maximum_bitcast_fusion = f32[32,16,2,64,16]{3,4,0,1,2:T(8,128)} fusion(f32[16,1,64,32,16]{2,4,3,0,1:T(8,128)} %bitcast.83, f32[16,1,64,32,16]{2,4,3,0,1:T(8,128)} %bitcast.82), kind=kLoop, calls=%fused_computation.5 | loop fusion | flops 1048576 | bytes 8388608 | tf_op jit(solution)/shard_map/transpose | solution.py:111
  312.8 13.4 %copy.91 = f32[32,16,2,64,16]{0,4,3,2,1:T(8,128)} copy(f32[32,16,2,64,16]{3,4,0,1,2:T(8,128)} %maximum_bitcast_fusion) | data formatting | bytes 8388608 | tf_op jit(solution)/shard_map/transpose | solution.py:111
  326.2 11.7 %copy.92 = f32[32,16,2,1024]{3,1,2,0:T(8,128)} copy(f32[32,16,2,1024]{0,3,2,1:T(8,128)} %bitcast.79) | data formatting | bytes 8388608 | tf_op jit(solution)/shard_map/reshape | solution.py:114
  337.9 5.5 %all-to-all-start.2 = ((f32[32,16,2,1024]{3,1,2,0:T(8,128)}), f32[32,16,2,1024]{3,1,2,0:T(8,128)}, u32[]{:S(2)}, u32[]{:S(2)}) async-start(f32[32,16,2,1024]{3,1,2,0:T(8,128)} %copy.92), calls=%async_computation.2 | async-start | bytes 8388608 | tf_op jit(solution)/shard_map/all_to_all | solution.py:115
  343.4 93.1 %all-to-all-done.2 = f32[32,16,2,1024]{3,1,2,0:T(8,128)} async-done(((f32[32,16,2,1024]{3,1,2,0:T(8,128)}), f32[32,16,2,1024]{3,1,2,0:T(8,128)}, u32[]{:S(2)}, u32[]{:S(2)}) %all-to-all-start.2) | async-done | bytes 4194336 | tf_op jit(solution)/shard_map/all_to_all | solution.py:115
  439.0 3.0 fusion.5
  442.1 3.0 fusion.6
  445.1 3.0 fusion.23
  448.1 3.2 fusion.24
  456.3 5.4 %copy.97 = f32[1024,2,512]{2,0,1:T(8,128)} copy(f32[1024,2,512]{0,2,1:T(8,128)} %fusion.4) | data formatting | bytes 8388608 | tf_op jit(solution)/shard_map/transpose | solution.py:127
  464.3 5.8 %copy.98 = f32[64,16,2,512]{3,2,1,0:T(2,128)} copy(f32[64,16,2,512]{3,1,0,2:T(8,128)S(1)} %broadcast_select_fusion) | data formatting | bytes 8388608 | tf_op jit(solution)/shard_map/jit(_where)/select_n | solution.py:131
  (35 shorter events, 40.8 us)
Async XLA Ops:
  63.8 195.1 %all-to-all-start.1 = ((bf16[8,16,64,512]{3,2,1,0:T(8,128)(2,1)}), bf16[8,16,64,512]{3,2,1,0:T(8,128)(2,1)}, u32[]{:S(2)}, u32[]{:S(2)}) async-start(bf16[8,16,64,512]{3,2,1,0:T(8,128)(2,1)} %stack.27), calls=%async_computation.1 | async-start | bytes 16777216 | tf_op jit(solution)/shard_map/all_to_all | solution.py:79
  271.8 5.8 %copy-start = (bf16[16,8,64,512]{3,2,1,0:T(8,128)(2,1)S(1)}, bf16[16,8,64,512]{3,2,1,0:T(8,128)(2,1)}, u32[]{:S(2)}) copy-start(bf16[16,8,64,512]{3,2,1,0:T(8,128)(2,1)} %copy.83) | copy-start | bytes 25165828
  337.9 98.6 %all-to-all-start.2 = ((f32[32,16,2,1024]{3,1,2,0:T(8,128)}), f32[32,16,2,1024]{3,1,2,0:T(8,128)}, u32[]{:S(2)}, u32[]{:S(2)}) async-start(f32[32,16,2,1024]{3,1,2,0:T(8,128)} %copy.92), calls=%async_computation.2 | async-start | bytes 8388608 | tf_op jit(solution)/shard_map/all_to_all | solution.py:115
